TPU v7x, 32 devices: a whole 2x2x4 slice. The times are simulated.
32 devices in a mesh: blk: 8 (over z, x), table: 4 (over y, core).
Axes of the slice: x: 2, y: 2, z: 4, core: 2. Of those that a mesh axis runs over, the one named last changes fastest.
Arguments:
- hot_slab: bfloat16 [128, 128], P('blk'), may hold values from -1.5 to 1.5
- hot_ids: int32 [4096, 16], P(('blk', 'table')), may hold values from 0 to 127
- dense: bfloat16 [4096, 128], P(('blk', 'table')), may hold values from -6 to 6
- cold_ids: int32 [4096, 26], P(('blk', 'table')), may hold values from 0 to 511
- table_slot: int32 [26], replicated, may hold values from 0 to 27, as said below
- cold_tables: bfloat16 [28, 512, 128], P('table'), may hold values from -6 to 6
- down_rank: bfloat16 [3456, 512], replicated, may hold values from -0.109375 to 0.109375
- up_rank: bfloat16 [512, 3456], replicated, may hold values from -0.25 to 0.25
- cross_bias: float32 [3456], replicated, may hold values from -3 to 3
- cotangent: bfloat16 [4096, 3456], P(('blk', 'table')), may hold values from -6 to 6
Outputs:
- crossed: bfloat16 [4096, 3456], P(('blk', 'table'))
- table_grad: float32 [8, 28, 512, 128], P('blk', 'table')
Inputs may be any that keep to these rules, and one draw needn't show every extreme that they name: `table_slot`: distinct values; some owner has all 7 of its slots taken.
All inputs are finite; a program needn't handle non-finite values.
Results may differ from a plain program's by a relative error of at most 0.0052.
Values may be sent and summed in bfloat16 or wider, within the bound.
No kernel may reach another device: no remote copies, remote signals or barrier semaphores. Data moves between devices by JAX's collectives and lax.ppermute only.
A program may use at most 64 MiB of HBM per device.

v0:
```python
import jax
import jax.numpy as jnp
from jax import lax
from jax.sharding import PartitionSpec as P


def bag_counts(row_ids, width_rows):
    positions = lax.broadcasted_iota(jnp.int32, (row_ids.shape[0], width_rows), 1)
    counts = jnp.zeros((row_ids.shape[0], width_rows), jnp.float32)
    for bag_index in range(row_ids.shape[1]):
        local_ids = row_ids[:, bag_index : bag_index + 1]
        counts = counts + (local_ids == positions).astype(jnp.float32)
    return counts.astype(jnp.bfloat16)


def on_device(
    hot_slab,
    hot_ids,
    dense,
    cold_ids,
    table_slot,
    cold_tables,
    down_rank,
    up_rank,
    cross_bias,
    cotangent,
):
    batch_rows = dense.shape[0]
    width = hot_slab.shape[1]
    table_count = table_slot.shape[0]
    owners = lax.axis_size("table")
    slots = cold_tables.shape[0]
    table_rows = cold_tables.shape[1]
    slot_total = owners * slots
    block_rows = lax.all_gather(hot_slab, "blk", axis=0, tiled=True)
    counts = bag_counts(hot_ids, block_rows.shape[0])
    pooled = jnp.dot(counts, block_rows, preferred_element_type=jnp.float32)
    front_row = (dense.astype(jnp.float32) + pooled).astype(jnp.bfloat16)
    slot_match = (
        table_slot[:, None] == lax.broadcasted_iota(jnp.int32, (table_count, slot_total), 1)
    ).astype(jnp.int32)
    send_ids = jnp.sum(cold_ids[:, :, None] * slot_match[None, :, :], axis=1).reshape(
        batch_rows, owners, slots
    )
    ids_block = lax.all_to_all(send_ids, "table", split_axis=1, concat_axis=1, tiled=True)
    item_count = ids_block.shape[0]
    row_count = item_count * ids_block.shape[1]
    columns = lax.broadcasted_iota(jnp.int32, (row_count, table_rows), 1)
    pieces = []
    for lookup_slot_index in range(slots):
        lookup_slot_ids = ids_block[:, :, lookup_slot_index].reshape(row_count, 1)
        lookup_selector = (lookup_slot_ids == columns).astype(jnp.bfloat16)
        rows_out = jnp.dot(
            lookup_selector, cold_tables[lookup_slot_index], preferred_element_type=jnp.float32
        )
        pieces.append(rows_out.astype(jnp.bfloat16).reshape(item_count, ids_block.shape[1], width))
    fetched_rows = jnp.stack(pieces, axis=2)
    returned = lax.all_to_all(fetched_rows, "table", split_axis=1, concat_axis=1, tiled=True)
    slot_pick = slot_match.astype(jnp.bfloat16)
    cold_rows = jnp.einsum(
        "skd,tk->std",
        returned.reshape(batch_rows, slot_total, width),
        slot_pick,
        preferred_element_type=jnp.float32,
    ).astype(jnp.bfloat16)
    feat_count = (table_count + 1) * width
    features = jnp.concatenate([front_row[:, None, :], cold_rows], axis=1).reshape(
        batch_rows, feat_count
    )
    low_rank = jnp.dot(features, down_rank, preferred_element_type=jnp.float32).astype(jnp.bfloat16)
    gate = jnp.dot(low_rank, up_rank, preferred_element_type=jnp.float32) + cross_bias[None, :]
    feat_wide = features.astype(jnp.float32)
    crossed = (feat_wide * gate + feat_wide).astype(jnp.bfloat16)
    cot_wide = cotangent.astype(jnp.float32)
    mixed = (cot_wide * feat_wide).astype(jnp.bfloat16)
    grad_low = jnp.dot(mixed, up_rank.T, preferred_element_type=jnp.float32).astype(jnp.bfloat16)
    grad_in = cot_wide * (gate + 1.0) + jnp.dot(
        grad_low, down_rank.T, preferred_element_type=jnp.float32
    )
    grad_in = grad_in.astype(jnp.bfloat16)
    grad_cold = grad_in.reshape(batch_rows, table_count + 1, width)[:, 1:, :]
    grad_slots = jnp.einsum("std,tk->skd", grad_cold, slot_pick, preferred_element_type=jnp.float32)
    grad_slots = grad_slots.astype(jnp.bfloat16).reshape(batch_rows, owners, slots, width)
    arrived = lax.all_to_all(grad_slots, "table", split_axis=1, concat_axis=1, tiled=True)
    row_positions = lax.broadcasted_iota(jnp.int32, (table_rows, batch_rows * owners), 0)
    slot_grads = []
    for slot_index in range(slots):
        slot_ids = ids_block[:, :, slot_index].reshape(1, batch_rows * owners)
        slot_rows = arrived[:, :, slot_index, :].reshape(batch_rows * owners, width)
        selector = (row_positions == slot_ids).astype(jnp.bfloat16)
        slot_grads.append(jnp.dot(selector, slot_rows, preferred_element_type=jnp.float32))
    table_grad = jnp.stack(slot_grads, axis=0)[None]
    return (crossed, table_grad)


def solution(mesh):
    placed = (
        P("blk", None),
        P(("blk", "table"), None),
        P(("blk", "table"), None),
        P(("blk", "table"), None),
        P(),
        P("table", None, None),
        P(),
        P(),
        P(),
        P(("blk", "table"), None),
    )
    return jax.shard_map(
        on_device,
        mesh=mesh,
        in_specs=placed,
        out_specs=(P(("blk", "table"), None), P("blk", "table", None, None)),
        check_vma=False,
    )
```

profile of v0, /device:TPU:0, one launch (start us, length us, event | category | flops | bytes accessed | tf_op | source)
XLA Modules:
  0.0 134.0 jit_solution(799297158164035277)
XLA Ops:
  0.6 1.4 %fusion.62 = s32[26,28]{0,1:T(8,128)} fusion(s32[26]{0:T(128)} %param.14), kind=kLoop, calls=%fused_computation.124 | loop fusion | flops 1456 | bytes 3016 | tf_op jit(solution)/shard_map/convert_element_type | solution.py:41
  2.9 1.5 %multiply_reduce_fusion = s32[128,28]{0,1:T(8,128)} fusion(s32[26,28]{1,0:T(8,128)S(1)} %copy.51, s32[128,26]{0,1:T(8,128)} %param.13), kind=kLoop, calls=%fused_computation.68 | loop fusion | flops 182784 | bytes 30560 | tf_op jit(solution)/shard_map/reduce_sum | solution.py:42
  5.1 7.9 %all_to_all.15 = s32[128,4,7]{0,2,1:T(8,128)S(1)} all-to-all(s32[128,4,7]{0,2,1:T(8,128)S(1)} %reshape.50), channel_id=1, replica_groups=mesh['blk'=8,'table'=4] {'table'}, dimensions={1} | all-to-all | bytes 28672 | tf_op jit(solution)/shard_map/all_to_all | solution.py:45
  13.6 1.4 %copy.58 = s32[128,4,1]{1,0,2:T(8,128)} copy(s32[128,4,1]{0,2,1:T(1,128)} %get-tuple-element.9) | data formatting | bytes 4096 | tf_op jit(solution)/shard_map/slice | solution.py:51
  15.0 1.5 %eq.366 = s32[512]{0:T(512)} reshape(s32[128,4,1]{1,0,2:T(8,128)} %copy.58) | data formatting | bytes 4096 | tf_op jit(solution)/shard_map/eq | solution.py:52
  16.5 1.4 %copy.57 = s32[128,4,1]{1,0,2:T(8,128)} copy(s32[128,4,1]{0,2,1:T(1,128)} %get-tuple-element.10) | data formatting | bytes 4096 | tf_op jit(solution)/shard_map/slice | solution.py:51
  17.9 1.5 %eq.363 = s32[512]{0:T(512)} reshape(s32[128,4,1]{1,0,2:T(8,128)} %copy.57) | data formatting | bytes 4096 | tf_op jit(solution)/shard_map/eq | solution.py:52
  19.5 1.4 %copy.56 = s32[128,4,1]{1,0,2:T(8,128)} copy(s32[128,4,1]{0,2,1:T(1,128)} %get-tuple-element.11) | data formatting | bytes 4096 | tf_op jit(solution)/shard_map/slice | solution.py:51
  20.9 1.5 %eq.360 = s32[512]{0:T(512)} reshape(s32[128,4,1]{1,0,2:T(8,128)} %copy.56) | data formatting | bytes 4096 | tf_op jit(solution)/shard_map/eq | solution.py:52
  23.1 1.5 %eq.357 = s32[512]{0:T(512)} reshape(s32[128,4,1]{1,0,2:T(8,128)} %copy.55) | data formatting | bytes 4096 | tf_op jit(solution)/shard_map/eq | solution.py:52
  25.4 1.5 %eq.354 = s32[512]{0:T(512)} reshape(s32[128,4,1]{1,0,2:T(8,128)} %copy.54) | data formatting | bytes 4096 | tf_op jit(solution)/shard_map/eq | solution.py:52
  29.4 1.5 %eq.348 = s32[512]{0:T(512)} reshape(s32[128,4,1]{1,0,2:T(8,128)} %copy.52) | data formatting | bytes 4096 | tf_op jit(solution)/shard_map/eq | solution.py:52
  30.9 1.3 convolution_convert_fusion.10
  33.4 1.3 convolution_convert_fusion.8
  34.7 1.3 convolution_convert_fusion.7
  37.3 1.3 convolution_convert_fusion.5
  44.6 4.2 %all-to-all-start.1 = ((bf16[128,4,7,128]{3,0,2,1:T(8,128)(2,1)}), bf16[128,4,7,128]{3,0,2,1:T(8,128)(2,1)}, u32[]{:S(2)}, u32[]{:S(2)}) async-start(bf16[128,4,7,128]{3,0,2,1:T(8,128)(2,1)} %copy_dynamic-update-slice_fusion), calls=%async_computation.1 | async-start | bytes 1835008 | tf_op jit(solution)/shard_map/all_to_all | solution.py:58
  48.8 1.5 %copy.50 = bf16[128,128]{0,1:T(8,128)(2,1)} copy(bf16[128,128]{1,0:T(8,128)(2,1)} %param.12) | data formatting | bytes 65536 | tf_op args[2]
  50.3 30.9 %all_gather.3 = bf16[128,128]{1,0:T(8,128)(2,1)S(1)} all-gather(bf16[16,128]{1,0:T(8,128)(2,1)S(1)} %copy-done.6), channel_id=1, replica_groups=mesh['blk'=8,'table'=4] {'blk'}, dimensions={0}, use_global_device_ids=true | all-gather | bytes 36864 | tf_op jit(solution)/shard_map/all_gather | solution.py:35
  81.2 1.9 %fusion.13 = bf16[128,1,128]{0,2,1:T(8,128)(2,1)} fusion(bf16[128,128]{1,0:T(8,128)(2,1)S(1)} %all_gather.3, bf16[128,128]{0,1:T(8,128)(2,1)} %copy.50, s32[128]{0:T(128)S(1)} %get-tuple-element.30, s32[128]{0:T(128)S(1)} %get-tuple-element.31, s32[128]{0:T(128)S(1)} %get-tuple-element.17, s32[128]{0:T(128)S(1)} %get-tuple-element.18, ...), kind=kOutput, calls=%fused_computation.37 | convolution fusion | flops 5029888 | bytes 106496 | tf_op jit(solution)/shard_map/dot_general | solution.py:37
  83.1 1.5 %copy.68 = bf16[128,1,128]{2,1,0:T(2,128)(2,1)} copy(bf16[128,1,128]{0,2,1:T(8,128)(2,1)} %fusion.13) | data formatting | bytes 65536 | tf_op jit(solution)/shard_map/broadcast_in_dim | solution.py:67
  84.6 1.9 %fusion.3 = bf16[128,26,128]{2,1,0:T(8,128)(2,1)S(1)} fusion(bf16[128,28,128]{2,0,1:T(8,128)(2,1)} %bitcast.32, s32[26]{0:T(128)S(1)} %copy-done.4), kind=kOutput, calls=%fused_computation.10 | convolution fusion | flops 24283272 | bytes 1769576 | tf_op jit(solution)/shard_map/skd,tk->std/dot_general | solution.py:60
  86.5 1.5 %pad_maximum_fusion = bf16[128,27,128]{2,1,0:T(8,128)(2,1)} fusion(bf16[128,26,128]{2,1,0:T(8,128)(2,1)S(1)} %fusion.3, bf16[128,1,128]{2,1,0:T(2,128)(2,1)S(1)} %copy-done.1), kind=kLoop, calls=%fused_computation.38 | loop fusion | flops 1769472 | bytes 1769472 | tf_op jit(solution)/shard_map/concatenate | solution.py:67
  88.0 2.6 %copy.69 = bf16[128,27,128]{0,2,1:T(8,128)(2,1)} copy(bf16[128,27,128]{2,1,0:T(8,128)(2,1)} %pad_maximum_fusion) | data formatting | bytes 1769472 | tf_op jit(solution)/shard_map/concatenate | solution.py:67
  90.6 2.2 %copy.70 = bf16[128,3456]{1,0:T(8,128)(2,1)} copy(bf16[128,3456]{0,1:T(8,128)(2,1)} %bitcast.142) | data formatting | bytes 1769472 | tf_op jit(solution)/shard_map/reshape | solution.py:67
  92.9 5.3 %fusion.2 = (bf16[128,3456]{1,0:T(8,128)(2,1)}, f32[128,3456]{1,0:T(8,128)}) fusion(bf16[128,3456]{1,0:T(8,128)(2,1)} %copy.70, f32[3456]{0:T(1024)S(1)} %copy-done.2, bf16[512,3456]{1,0:T(8,128)(2,1)S(1)} %copy-done, bf16[128,3456]{0,1:T(8,128)(2,1)} %bitcast.143, bf16[3456,512]{1,0:T(8,128)(2,1)} %param.16), kind=kOutput, calls=%fused_computation.7 | convolution fusion | flops 908247040 | bytes 11515392 | tf_op jit(solution)/shard_map/dot_general | solution.py:71
  98.2 6.3 %fusion = bf16[128,3456]{1,0:T(8,128)(2,1)} fusion(bf16[3456,512]{1,0:T(8,128)(2,1)} %param.16, bf16[128,3456]{1,0:T(8,128)(2,1)} %param.19, f32[128,3456]{1,0:T(8,128)} %get-tuple-element.33, bf16[512,3456]{1,0:T(8,128)(2,1)S(1)} %copy-done, bf16[128,3456]{1,0:T(8,128)(2,1)} %copy.70), kind=kOutput, calls=%fused_computation.2 | convolution fusion | flops 910016512 | bytes 11501568 | tf_op jit(solution)/shard_map/dot_general | solution.py:77
  104.5 2.2 %copy.71 = bf16[128,3456]{0,1:T(8,128)(2,1)} copy(bf16[128,3456]{1,0:T(8,128)(2,1)} %fusion) | data formatting | bytes 1769472 | tf_op jit(solution)/shard_map/convert_element_type | solution.py:80
  106.7 2.2 %slice.166 = bf16[128,26,128]{0,2,1:T(8,128)(2,1)} slice(bf16[128,27,128]{0,2,1:T(8,128)(2,1)} %bitcast.145), slice={[0:128], [1:27], [0:128]} | slice | bytes 1703936 | tf_op jit(solution)/shard_map/slice | solution.py:81
  108.9 2.6 %copy.83 = bf16[128,26,128]{2,1,0:T(8,128)(2,1)} copy(bf16[128,26,128]{0,2,1:T(8,128)(2,1)} %slice.166) | data formatting | bytes 1703936
  111.5 1.6 %fusion.4 = bf16[128,28,128]{2,1,0:T(8,128)(2,1)S(1)} fusion(bf16[128,26,128]{2,1,0:T(8,128)(2,1)} %copy.83, s32[26]{0:T(128)S(1)} %copy-done.5), kind=kOutput, calls=%fused_computation.11 | convolution fusion | flops 24316040 | bytes 1769576 | tf_op jit(solution)/shard_map/std,tk->skd/dot_general | solution.py:82
  113.5 16.1 %all_to_all.16 = bf16[128,4,7,128]{3,0,2,1:T(8,128)(2,1)S(1)} all-to-all(bf16[128,4,7,128]{3,0,2,1:T(8,128)(2,1)S(1)} %bitcast.144), channel_id=1, replica_groups=mesh['blk'=8,'table'=4] {'table'}, dimensions={1} | all-to-all | bytes 1835008 | tf_op jit(solution)/shard_map/all_to_all | solution.py:84
  (74 shorter events, 19.2 us)
Async XLA Ops:
  0.6 92.2 %copy-start = (bf16[512,3456]{1,0:T(8,128)(2,1)S(1)}, bf16[512,3456]{1,0:T(8,128)(2,1)}, u32[]{:S(2)}) copy-start(bf16[512,3456]{1,0:T(8,128)(2,1)} %param.17) | copy-start | bytes 10616836
  23.1 12.9 %copy-start.10 = (s32[512]{0:T(512)S(1)}, s32[512]{0:T(512)}, u32[]{:S(2)}) copy-start(s32[512]{0:T(512)} %eq.360) | copy-start | bytes 6148
  25.4 9.3 %copy-start.12 = (s32[512]{0:T(512)S(1)}, s32[512]{0:T(512)}, u32[]{:S(2)}) copy-start(s32[512]{0:T(512)} %eq.357) | copy-start | bytes 6148
  28.6 9.9 %copy-start.15 = (s32[512]{0:T(512)}, s32[512]{0:T(512)S(1)}, u32[]{:S(2)}) copy-start(s32[512]{0:T(512)S(1)} %eq.351) | copy-start | bytes 6148
  29.4 9.2 %copy-start.7 = (s32[512]{0:T(512)S(1)}, s32[512]{0:T(512)}, u32[]{:S(2)}) copy-start(s32[512]{0:T(512)} %eq.366) | copy-start | bytes 6148
  39.8 10.5 %copy-start.6 = (bf16[16,128]{1,0:T(8,128)(2,1)S(1)}, bf16[16,128]{1,0:T(8,128)(2,1)}, u32[]{:S(2)}) copy-start(bf16[16,128]{1,0:T(8,128)(2,1)} %param.10) | copy-start | bytes 12292
  39.8 41.4 %copy-start.3 = (s32[128,16]{0,1:T(8,128)S(1)}, s32[128,16]{0,1:T(8,128)}, u32[]{:S(2)}) copy-start(s32[128,16]{0,1:T(8,128)} %param.11) | copy-start | bytes 24580
  43.2 41.4 %copy-start.4 = (s32[26]{0:T(128)S(1)}, s32[26]{0:T(128)}, u32[]{:S(2)}) copy-start(s32[26]{0:T(128)} %param.14) | copy-start | bytes 316
  44.6 40.0 %all-to-all-start.1 = ((bf16[128,4,7,128]{3,0,2,1:T(8,128)(2,1)}), bf16[128,4,7,128]{3,0,2,1:T(8,128)(2,1)}, u32[]{:S(2)}, u32[]{:S(2)}) async-start(bf16[128,4,7,128]{3,0,2,1:T(8,128)(2,1)} %copy_dynamic-update-slice_fusion), calls=%async_computation.1 | async-start | bytes 1835008 | tf_op jit(solution)/shard_map/all_to_all | solution.py:58
  84.6 1.9 %copy-start.1 = (bf16[128,1,128]{2,1,0:T(2,128)(2,1)S(1)}, bf16[128,1,128]{2,1,0:T(2,128)(2,1)}, u32[]{:S(2)}) copy-start(bf16[128,1,128]{2,1,0:T(2,128)(2,1)} %copy.68) | copy-start | bytes 98308
  88.0 4.8 %copy-start.2 = (f32[3456]{0:T(1024)S(1)}, f32[3456]{0:T(1024)}, u32[]{:S(2)}) copy-start(f32[3456]{0:T(1024)} %param.18) | copy-start | bytes 41476
  106.7 4.8 %copy-start.5 = (s32[26]{0:T(128)S(1)}, s32[26]{0:T(128)}, u32[]{:S(2)}) copy-start(s32[26]{0:T(128)} %param.14) | copy-start | bytes 316
  129.6 0.9 copy-start.17
  129.6 1.3 copy-start.16
  129.7 1.5 %copy-start.14 = (s32[512]{0:T(512)S(1)}, s32[512]{0:T(512)}, u32[]{:S(2)}) copy-start(s32[512]{0:T(512)} %eq.354) | copy-start | bytes 6148
  129.7 1.8 %copy-start.13 = (s32[512]{0:T(512)S(1)}, s32[512]{0:T(512)}, u32[]{:S(2)}) copy-start(s32[512]{0:T(512)} %eq.357) | copy-start | bytes 6148
  129.9 1.9 %copy-start.11 = (s32[512]{0:T(512)S(1)}, s32[512]{0:T(512)}, u32[]{:S(2)}) copy-start(s32[512]{0:T(512)} %eq.360) | copy-start | bytes 6148
  130.2 2.0 %copy-start.9 = (s32[512]{0:T(512)S(1)}, s32[512]{0:T(512)}, u32[]{:S(2)}) copy-start(s32[512]{0:T(512)} %eq.363) | copy-start | bytes 6148
  130.4 2.0 %copy-start.8 = (s32[512]{0:T(512)S(1)}, s32[512]{0:T(512)}, u32[]{:S(2)}) copy-start(s32[512]{0:T(512)} %eq.366) | copy-start | bytes 6148
  132.8 1.2 copy-start.18
where the time goes:
time: 135 us; the launch traced here: 134 us
  blocking collectives  54.9 us (41%)
  local copies, waits for them, and re-layouts  41.4 us (31%)
  matrix products  28 us (21%)
  other arithmetic  4.39 us (3%)
  starting transfers between devices  4.22 us (3%)
    all_gather x1, blocking collectives, on_device(): block_rows = lax.all_gather(hot_slab, 'blk', axis=0, tiled=True)  30.9 us
    all_to_all x1, blocking collectives, on_device(): lax.all_to_all(grad_slots, 'table', split_axis=1, concat_axis=1, tiled=True)  16.1 us
    eq x7, local copies, waits for them, and re-layouts, on_device(): lookup_selector = (lookup_slot_ids == columns).astype(jnp.bfloat16)  10.1 us
    unnamed x46, local copies, waits for them, and re-layouts  9.46 us
    dot_general x7, matrix products, on_device(): jnp.dot(lookup_selector, cold_tables[lookup_slot_index], preferred_elemen...  8.85 us
    all_to_all x1, blocking collectives, on_device(): lax.all_to_all(send_ids, 'table', split_axis=1, concat_axis=1, tiled=True)  7.91 us
    slice x8, local copies, waits for them, and re-layouts, on_device(): lookup_slot_ids = ids_block[:, :, lookup_slot_index].reshape(row_count, 1)  7.77 us
    dot_general x1, matrix products, on_device(): jnp.dot(grad_low, down_rank.T, preferred_element_type=jnp.float32)  6.33 us
  transfers between devices with their start and end apart: 1, of which 0 were waited for; matrix products, arithmetic and copies ran while one was open for 4% of the time, Pallas kernels for 0%

commit v1 on v0

--- a/solution.py
+++ b/solution.py
@@ -32,7 +32,15 @@
     slots = cold_tables.shape[0]
     table_rows = cold_tables.shape[1]
     slot_total = owners * slots
-    block_rows = lax.all_gather(hot_slab, "blk", axis=0, tiled=True)
+    ways, here = (lax.axis_size("blk"), lax.axis_index("blk"))
+    grown, reach = (hot_slab, 1)
+    while reach < ways:
+        theirs = lax.ppermute(grown, "blk", [(d, d ^ reach) for d in range(ways)])
+        mine_first = jnp.concatenate([grown, theirs], axis=0)
+        theirs_first = jnp.concatenate([theirs, grown], axis=0)
+        grown = jnp.where(here & reach == 0, mine_first, theirs_first)
+        reach = 2 * reach
+    block_rows = grown
     counts = bag_counts(hot_ids, block_rows.shape[0])
     pooled = jnp.dot(counts, block_rows, preferred_element_type=jnp.float32)
     front_row = (dense.astype(jnp.float32) + pooled).astype(jnp.bfloat16)

time: 135 us -> 118 us (0.87)
  blocking collectives: 54.9 us -> 23.9 us
  starting transfers between devices: 4.22 us -> 9.94 us
  waiting for transfers between devices: 0.01 us -> 4.66 us
  other arithmetic: 4.39 us -> 6.54 us
    all_gather x1 -> x0, blocking collectives: 30.9 us -> none  [on_device(): block_rows = lax.all_gather(hot_slab, 'blk', axis=0, tiled=True)]
    ppermute x0 -> x3, starting transfers between devices: none -> 5.72 us  [on_device(): theirs = lax.ppermute(grown, 'blk', [(d, d ^ reach) for d in range(ways)])]
    ppermute x0 -> x3, waiting for transfers between devices: none -> 4.66 us  [on_device(): theirs = lax.ppermute(grown, 'blk', [(d, d ^ reach) for d in range(ways)])]
    select_n x0 -> x2, other arithmetic: none -> 2.15 us  [on_device(): grown = jnp.where(here & reach == 0, mine_first, theirs_first)]
    unnamed x46 -> x44, local copies, waits for them, and re-layouts: 9.46 us -> 9.46 us
  transfers between devices with their start and end apart: 1 -> 4, of which waited for: 0 -> 3; matrix products, arithmetic and copies ran while one was open for 4% -> 7% of each run, Pallas kernels for 0% -> 0%
where the time goes in v1:
time: 118 us; the launch traced here: 116 us
  local copies, waits for them, and re-layouts  42.1 us (36%)
  matrix products  28.1 us (24%)
  blocking collectives  23.9 us (20%)
  starting transfers between devices  9.94 us (8%)
  other arithmetic  6.54 us (6%)
  waiting for transfers between devices  4.66 us (4%)
    all_to_all x1, blocking collectives, on_device(): lax.all_to_all(grad_slots, 'table', split_axis=1, concat_axis=1, tiled=True)  16 us
    eq x7, local copies, waits for them, and re-layouts, on_device(): lookup_selector = (lookup_slot_ids == columns).astype(jnp.bfloat16)  10.1 us
    unnamed x44, local copies, waits for them, and re-layouts  9.46 us
    dot_general x7, matrix products, on_device(): jnp.dot(lookup_selector, cold_tables[lookup_slot_index], preferred_elemen...  8.85 us
    all_to_all x1, blocking collectives, on_device(): lax.all_to_all(send_ids, 'table', split_axis=1, concat_axis=1, tiled=True)  7.91 us
    slice x8, local copies, waits for them, and re-layouts, on_device(): lookup_slot_ids = ids_block[:, :, lookup_slot_index].reshape(row_count, 1)  7.78 us
    dot_general x1, matrix products, on_device(): jnp.dot(grad_low, down_rank.T, preferred_element_type=jnp.float32)  6.31 us
    ppermute x3, starting transfers between devices, on_device(): theirs = lax.ppermute(grown, 'blk', [(d, d ^ reach) for d in range(ways)])  5.72 us
  transfers between devices with their start and end apart: 4, of which 3 were waited for; matrix products, arithmetic and copies ran while one was open for 7% of the time, Pallas kernels for 0%

profile of v1, /device:TPU:0, one launch (start us, length us, event | category | flops | bytes accessed | tf_op | source)
XLA Modules:
  0.0 116.3 jit_solution(8942580780831170309)
XLA Ops:
  0.6 1.4 %fusion.68 = s32[26,28]{0,1:T(8,128)} fusion(s32[26]{0:T(128)} %param.14), kind=kLoop, calls=%fused_computation.132 | loop fusion | flops 1456 | bytes 3016 | tf_op jit(solution)/shard_map/convert_element_type | solution.py:49
  2.9 1.5 %multiply_reduce_fusion = s32[128,28]{0,1:T(8,128)} fusion(s32[26,28]{1,0:T(8,128)S(1)} %copy.51, s32[128,26]{0,1:T(8,128)} %param.13), kind=kLoop, calls=%fused_computation.68 | loop fusion | flops 182784 | bytes 30560 | tf_op jit(solution)/shard_map/reduce_sum | solution.py:50
  5.1 7.9 %all_to_all.15 = s32[128,4,7]{0,2,1:T(8,128)S(1)} all-to-all(s32[128,4,7]{0,2,1:T(8,128)S(1)} %reshape.50), channel_id=1, replica_groups=mesh['blk'=8,'table'=4] {'table'}, dimensions={1} | all-to-all | bytes 28672 | tf_op jit(solution)/shard_map/all_to_all | solution.py:53
  13.6 1.4 %copy.58 = s32[128,4,1]{1,0,2:T(8,128)} copy(s32[128,4,1]{0,2,1:T(1,128)} %get-tuple-element.9) | data formatting | bytes 4096 | tf_op jit(solution)/shard_map/slice | solution.py:59
  15.0 1.5 %eq.378 = s32[512]{0:T(512)} reshape(s32[128,4,1]{1,0,2:T(8,128)} %copy.58) | data formatting | bytes 4096 | tf_op jit(solution)/shard_map/eq | solution.py:60
  16.5 1.4 %copy.57 = s32[128,4,1]{1,0,2:T(8,128)} copy(s32[128,4,1]{0,2,1:T(1,128)} %get-tuple-element.10) | data formatting | bytes 4096 | tf_op jit(solution)/shard_map/slice | solution.py:59
  17.9 1.5 %eq.375 = s32[512]{0:T(512)} reshape(s32[128,4,1]{1,0,2:T(8,128)} %copy.57) | data formatting | bytes 4096 | tf_op jit(solution)/shard_map/eq | solution.py:60
  19.5 1.4 %copy.56 = s32[128,4,1]{1,0,2:T(8,128)} copy(s32[128,4,1]{0,2,1:T(1,128)} %get-tuple-element.11) | data formatting | bytes 4096 | tf_op jit(solution)/shard_map/slice | solution.py:59
  20.9 1.5 %eq.372 = s32[512]{0:T(512)} reshape(s32[128,4,1]{1,0,2:T(8,128)} %copy.56) | data formatting | bytes 4096 | tf_op jit(solution)/shard_map/eq | solution.py:60
  23.1 1.5 %eq.369 = s32[512]{0:T(512)} reshape(s32[128,4,1]{1,0,2:T(8,128)} %copy.55) | data formatting | bytes 4096 | tf_op jit(solution)/shard_map/eq | solution.py:60
  25.4 1.5 %eq.366 = s32[512]{0:T(512)} reshape(s32[128,4,1]{1,0,2:T(8,128)} %copy.54) | data formatting | bytes 4096 | tf_op jit(solution)/shard_map/eq | solution.py:60
  29.4 1.5 %eq.360 = s32[512]{0:T(512)} reshape(s32[128,4,1]{1,0,2:T(8,128)} %copy.52) | data formatting | bytes 4096 | tf_op jit(solution)/shard_map/eq | solution.py:60
  44.6 4.2 %all-to-all-start.1 = ((bf16[128,4,7,128]{3,0,2,1:T(8,128)(2,1)}), bf16[128,4,7,128]{3,0,2,1:T(8,128)(2,1)}, u32[]{:S(2)}, u32[]{:S(2)}) async-start(bf16[128,4,7,128]{3,0,2,1:T(8,128)(2,1)} %copy_dynamic-update-slice_fusion), calls=%async_computation.1 | async-start | bytes 1835008 | tf_op jit(solution)/shard_map/all_to_all | solution.py:66
  48.8 1.6 %collective-permute-start = (bf16[16,128]{1,0:T(8,128)(2,1)S(1)}, bf16[16,128]{1,0:T(8,128)(2,1)}, u32[]{:S(2)}, u32[]{:S(2)}) collective-permute-start(bf16[16,128]{1,0:T(8,128)(2,1)S(1)} %copy-done.5), channel_id=1, source_target_pairs={{0,4},{4,0},{8,12},{12,8},{16,20},{20,16},{24,28},{28,24},{1,5},{5... | collective-permute-start | bytes 12296 | tf_op jit(solution)/shard_map/ppermute | solution.py:38
  50.4 2.2 %collective-permute-done = bf16[16,128]{1,0:T(8,128)(2,1)} collective-permute-done((bf16[16,128]{1,0:T(8,128)(2,1)S(1)}, bf16[16,128]{1,0:T(8,128)(2,1)}, u32[]{:S(2)}, u32[]{:S(2)}) %collective-permute-start) | collective-permute-done | bytes 4128 | tf_op jit(solution)/shard_map/ppermute | solution.py:38
  53.4 1.6 %collective-permute-start.1 = (bf16[32,128]{1,0:T(8,128)(2,1)S(1)}, bf16[32,128]{1,0:T(8,128)(2,1)}, u32[]{:S(2)}, u32[]{:S(2)}) collective-permute-start(bf16[32,128]{1,0:T(8,128)(2,1)S(1)} %maximum_select_fusion.3), channel_id=1, source_target_pairs={{0,8},{4,12},{8,0},{12,4},{16,24},{20,28},{24,16},{28,20},{1,9},{5... | collective-permute-start | bytes 24584 | tf_op jit(solution)/shard_map/ppermute | solution.py:38
  54.9 2.2 %collective-permute-done.1 = bf16[32,128]{1,0:T(8,128)(2,1)} collective-permute-done((bf16[32,128]{1,0:T(8,128)(2,1)S(1)}, bf16[32,128]{1,0:T(8,128)(2,1)}, u32[]{:S(2)}, u32[]{:S(2)}) %collective-permute-start.1) | collective-permute-done | bytes 8224 | tf_op jit(solution)/shard_map/ppermute | solution.py:38
  58.5 2.6 %collective-permute-start.2 = (bf16[64,128]{1,0:T(8,128)(2,1)}, bf16[64,128]{1,0:T(8,128)(2,1)}, u32[]{:S(2)}, u32[]{:S(2)}) collective-permute-start(bf16[64,128]{1,0:T(8,128)(2,1)} %maximum_select_fusion.2), channel_id=1, source_target_pairs={{0,16},{4,20},{8,24},{12,28},{16,0},{20,4},{24,8},{28,12},{1,17},{... | collective-permute-start | bytes 49160 | tf_op jit(solution)/shard_map/ppermute | solution.py:38
  61.7 1.5 %copy.50 = bf16[128,128]{0,1:T(8,128)(2,1)} copy(bf16[128,128]{1,0:T(8,128)(2,1)} %param.12) | data formatting | bytes 65536 | tf_op args[2]
  63.5 1.9 %fusion.13 = bf16[128,1,128]{0,2,1:T(8,128)(2,1)} fusion(bf16[128,128]{0,1:T(8,128)(2,1)} %copy.50, bf16[64,128]{1,0:T(8,128)(2,1)} %collective-permute-done.2, bf16[64,128]{1,0:T(8,128)(2,1)} %maximum_select_fusion.2, s32[128]{0:T(128)} %get-tuple-element.30, s32[128]{0:T(128)} %get-tuple-element.31, s32[128]{0:T(128)S(1)} %get-tuple-element.17, ...), kind=kOutput, calls=%fused_computation.37 | convolution fusion | flops 5177344 | bytes 106497 | tf_op jit(solution)/shard_map/dot_general | solution.py:45
  65.4 1.5 %copy.68 = bf16[128,1,128]{2,1,0:T(2,128)(2,1)} copy(bf16[128,1,128]{0,2,1:T(8,128)(2,1)} %fusion.13) | data formatting | bytes 65536 | tf_op jit(solution)/shard_map/broadcast_in_dim | solution.py:75
  66.9 1.9 %fusion.3 = bf16[128,26,128]{2,1,0:T(8,128)(2,1)S(1)} fusion(bf16[128,28,128]{2,0,1:T(8,128)(2,1)} %bitcast.32, s32[26]{0:T(128)} %param.14), kind=kOutput, calls=%fused_computation.10 | convolution fusion | flops 24283272 | bytes 1769576 | tf_op jit(solution)/shard_map/skd,tk->std/dot_general | solution.py:68
  68.9 1.5 %pad_maximum_fusion = bf16[128,27,128]{2,1,0:T(8,128)(2,1)} fusion(bf16[128,26,128]{2,1,0:T(8,128)(2,1)S(1)} %fusion.3, bf16[128,1,128]{2,1,0:T(2,128)(2,1)S(1)} %copy-done.1), kind=kLoop, calls=%fused_computation.38 | loop fusion | flops 1769472 | bytes 1769472 | tf_op jit(solution)/shard_map/concatenate | solution.py:75
  70.3 2.6 %copy.69 = bf16[128,27,128]{0,2,1:T(8,128)(2,1)} copy(bf16[128,27,128]{2,1,0:T(8,128)(2,1)} %pad_maximum_fusion) | data formatting | bytes 1769472 | tf_op jit(solution)/shard_map/concatenate | solution.py:75
  72.9 2.3 %copy.70 = bf16[128,3456]{1,0:T(8,128)(2,1)} copy(bf16[128,3456]{0,1:T(8,128)(2,1)} %bitcast.141) | data formatting | bytes 1769472 | tf_op jit(solution)/shard_map/reshape | solution.py:75
  75.2 5.3 %fusion.2 = (bf16[128,3456]{1,0:T(8,128)(2,1)}, f32[128,3456]{1,0:T(8,128)}) fusion(bf16[128,3456]{1,0:T(8,128)(2,1)} %copy.70, f32[3456]{0:T(1024)S(1)} %copy-done.2, bf16[512,3456]{1,0:T(8,128)(2,1)S(1)} %copy-done, bf16[128,3456]{0,1:T(8,128)(2,1)} %bitcast.142, bf16[3456,512]{1,0:T(8,128)(2,1)} %param.16), kind=kOutput, calls=%fused_computation.7 | convolution fusion | flops 908247040 | bytes 11515392 | tf_op jit(solution)/shard_map/dot_general | solution.py:79
  80.5 6.3 %fusion = bf16[128,3456]{1,0:T(8,128)(2,1)} fusion(bf16[3456,512]{1,0:T(8,128)(2,1)} %param.16, bf16[128,3456]{1,0:T(8,128)(2,1)} %param.19, f32[128,3456]{1,0:T(8,128)} %get-tuple-element.33, bf16[512,3456]{1,0:T(8,128)(2,1)S(1)} %copy-done, bf16[128,3456]{1,0:T(8,128)(2,1)} %copy.70), kind=kOutput, calls=%fused_computation.2 | convolution fusion | flops 910016512 | bytes 11501568 | tf_op jit(solution)/shard_map/dot_general | solution.py:85
  86.8 2.2 %copy.71 = bf16[128,3456]{0,1:T(8,128)(2,1)} copy(bf16[128,3456]{1,0:T(8,128)(2,1)} %fusion) | data formatting | bytes 1769472 | tf_op jit(solution)/shard_map/convert_element_type | solution.py:88
  89.0 2.2 %slice.166 = bf16[128,26,128]{0,2,1:T(8,128)(2,1)} slice(bf16[128,27,128]{0,2,1:T(8,128)(2,1)} %bitcast.144), slice={[0:128], [1:27], [0:128]} | slice | bytes 1703936 | tf_op jit(solution)/shard_map/slice | solution.py:89
  91.2 2.6 %copy.83 = bf16[128,26,128]{2,1,0:T(8,128)(2,1)} copy(bf16[128,26,128]{0,2,1:T(8,128)(2,1)} %slice.166) | data formatting | bytes 1703936
  93.8 1.6 %fusion.4 = bf16[128,28,128]{2,1,0:T(8,128)(2,1)S(1)} fusion(bf16[128,26,128]{2,1,0:T(8,128)(2,1)} %copy.83, s32[26]{0:T(128)S(1)} %copy-done.4), kind=kOutput, calls=%fused_computation.11 | convolution fusion | flops 24316040 | bytes 1769576 | tf_op jit(solution)/shard_map/std,tk->skd/dot_general | solution.py:90
  95.8 16.0 %all_to_all.16 = bf16[128,4,7,128]{3,0,2,1:T(8,128)(2,1)S(1)} all-to-all(bf16[128,4,7,128]{3,0,2,1:T(8,128)(2,1)S(1)} %bitcast.143), channel_id=1, replica_groups=mesh['blk'=8,'table'=4] {'table'}, dimensions={1} | all-to-all | bytes 1835008 | tf_op jit(solution)/shard_map/all_to_all | solution.py:92
  (79 shorter events, 27.3 us)
Async XLA Ops:
  0.6 74.6 %copy-start = (bf16[512,3456]{1,0:T(8,128)(2,1)S(1)}, bf16[512,3456]{1,0:T(8,128)(2,1)}, u32[]{:S(2)}) copy-start(bf16[512,3456]{1,0:T(8,128)(2,1)} %param.17) | copy-start | bytes 10616836
  23.1 12.9 %copy-start.9 = (s32[512]{0:T(512)S(1)}, s32[512]{0:T(512)}, u32[]{:S(2)}) copy-start(s32[512]{0:T(512)} %eq.372) | copy-start | bytes 6148
  25.4 9.3 %copy-start.11 = (s32[512]{0:T(512)S(1)}, s32[512]{0:T(512)}, u32[]{:S(2)}) copy-start(s32[512]{0:T(512)} %eq.369) | copy-start | bytes 6148
  28.6 9.9 %copy-start.14 = (s32[512]{0:T(512)}, s32[512]{0:T(512)S(1)}, u32[]{:S(2)}) copy-start(s32[512]{0:T(512)S(1)} %eq.363) | copy-start | bytes 6148
  29.4 9.2 %copy-start.6 = (s32[512]{0:T(512)S(1)}, s32[512]{0:T(512)}, u32[]{:S(2)}) copy-start(s32[512]{0:T(512)} %eq.378) | copy-start | bytes 6148
  39.8 9.0 %copy-start.5 = (bf16[16,128]{1,0:T(8,128)(2,1)S(1)}, bf16[16,128]{1,0:T(8,128)(2,1)}, u32[]{:S(2)}) copy-start(bf16[16,128]{1,0:T(8,128)(2,1)} %param.10) | copy-start | bytes 12292
  39.9 21.2 %copy-start.3 = (s32[128,16]{0,1:T(8,128)S(1)}, s32[128,16]{0,1:T(8,128)}, u32[]{:S(2)}) copy-start(s32[128,16]{0,1:T(8,128)} %param.11) | copy-start | bytes 24580
  44.6 22.3 %all-to-all-start.1 = ((bf16[128,4,7,128]{3,0,2,1:T(8,128)(2,1)}), bf16[128,4,7,128]{3,0,2,1:T(8,128)(2,1)}, u32[]{:S(2)}, u32[]{:S(2)}) async-start(bf16[128,4,7,128]{3,0,2,1:T(8,128)(2,1)} %copy_dynamic-update-slice_fusion), calls=%async_computation.1 | async-start | bytes 1835008 | tf_op jit(solution)/shard_map/all_to_all | solution.py:66
  48.8 3.8 %collective-permute-start = (bf16[16,128]{1,0:T(8,128)(2,1)S(1)}, bf16[16,128]{1,0:T(8,128)(2,1)}, u32[]{:S(2)}, u32[]{:S(2)}) collective-permute-start(bf16[16,128]{1,0:T(8,128)(2,1)S(1)} %copy-done.5), channel_id=1, source_target_pairs={{0,4},{4,0},{8,12},{12,8},{16,20},{20,16},{24,28},{28,24},{1,5},{5... | collective-permute-start | bytes 12296 | tf_op jit(solution)/shard_map/ppermute | solution.py:38
  53.4 3.8 %collective-permute-start.1 = (bf16[32,128]{1,0:T(8,128)(2,1)S(1)}, bf16[32,128]{1,0:T(8,128)(2,1)}, u32[]{:S(2)}, u32[]{:S(2)}) collective-permute-start(bf16[32,128]{1,0:T(8,128)(2,1)S(1)} %maximum_select_fusion.3), channel_id=1, source_target_pairs={{0,8},{4,12},{8,0},{12,4},{16,24},{20,28},{24,16},{28,20},{1,9},{5... | collective-permute-start | bytes 24584 | tf_op jit(solution)/shard_map/ppermute | solution.py:38
  58.5 5.0 %collective-permute-start.2 = (bf16[64,128]{1,0:T(8,128)(2,1)}, bf16[64,128]{1,0:T(8,128)(2,1)}, u32[]{:S(2)}, u32[]{:S(2)}) collective-permute-start(bf16[64,128]{1,0:T(8,128)(2,1)} %maximum_select_fusion.2), channel_id=1, source_target_pairs={{0,16},{4,20},{8,24},{12,28},{16,0},{20,4},{24,8},{28,12},{1,17},{... | collective-permute-start | bytes 49160 | tf_op jit(solution)/shard_map/ppermute | solution.py:38
  66.9 1.9 %copy-start.1 = (bf16[128,1,128]{2,1,0:T(2,128)(2,1)S(1)}, bf16[128,1,128]{2,1,0:T(2,128)(2,1)}, u32[]{:S(2)}) copy-start(bf16[128,1,128]{2,1,0:T(2,128)(2,1)} %copy.68) | copy-start | bytes 98308
  70.3 4.9 %copy-start.2 = (f32[3456]{0:T(1024)S(1)}, f32[3456]{0:T(1024)}, u32[]{:S(2)}) copy-start(f32[3456]{0:T(1024)} %param.18) | copy-start | bytes 41476
  89.0 4.8 %copy-start.4 = (s32[26]{0:T(128)S(1)}, s32[26]{0:T(128)}, u32[]{:S(2)}) copy-start(s32[26]{0:T(128)} %param.14) | copy-start | bytes 316
  111.9 0.9 copy-start.16
  111.9 1.3 %copy-start.15 = (s32[512]{0:T(512)S(1)}, s32[512]{0:T(512)}, u32[]{:S(2)}) copy-start(s32[512]{0:T(512)} %copy-done.14) | copy-start | bytes 6148
  111.9 1.5 %copy-start.13 = (s32[512]{0:T(512)S(1)}, s32[512]{0:T(512)}, u32[]{:S(2)}) copy-start(s32[512]{0:T(512)} %eq.366) | copy-start | bytes 6148
  112.0 1.8 %copy-start.12 = (s32[512]{0:T(512)S(1)}, s32[512]{0:T(512)}, u32[]{:S(2)}) copy-start(s32[512]{0:T(512)} %eq.369) | copy-start | bytes 6148
  112.2 1.9 %copy-start.10 = (s32[512]{0:T(512)S(1)}, s32[512]{0:T(512)}, u32[]{:S(2)}) copy-start(s32[512]{0:T(512)} %eq.372) | copy-start | bytes 6148
  112.4 2.0 %copy-start.8 = (s32[512]{0:T(512)S(1)}, s32[512]{0:T(512)}, u32[]{:S(2)}) copy-start(s32[512]{0:T(512)} %eq.375) | copy-start | bytes 6148
  112.7 2.0 %copy-start.7 = (s32[512]{0:T(512)S(1)}, s32[512]{0:T(512)}, u32[]{:S(2)}) copy-start(s32[512]{0:T(512)} %eq.378) | copy-start | bytes 6148
  115.0 1.2 %copy-start.17 = (f32[7,512,128]{2,1,0:T(8,128)}, f32[7,512,128]{2,1,0:T(8,128)S(1)}, u32[]{:S(2)}) copy-start(f32[7,512,128]{2,1,0:T(8,128)S(1)} %fusion.5) | copy-start | bytes 5505028
